TPU v7x, 512 devices: a whole 4x8x8 slice. The times are simulated.
512 devices in a mesh: rep: 64 (over z_hi, y, core), fsdp: 8 (over x, z_lo).
Axes of the slice: x: 4, y: 8, z: 8 (z_hi: 4, z_lo: 2; z = z_hi * 2 + z_lo), core: 2. Of those that a mesh axis runs over, the one named last changes fastest.
Arguments:
- anchor: float32 [4096, 512], P('fsdp', 'rep'), may hold values from -6 to 6
- momentum: float32 [4096, 512], P('fsdp', 'rep'), may hold values from -1.2 to 1.2
- tokens: bfloat16 [64, 2048, 4096], P('rep', 'fsdp'), may hold values from -6 to 6
- targets: bfloat16 [64, 2048, 512], P('rep', 'fsdp'), may hold values from -6 to 6
- first_moment: float32 [64, 4096, 512], P('rep', 'fsdp'), may hold values from -0.0018 to 0.0018
- second_moment: float32 [64, 4096, 512], P('rep', 'fsdp'), may hold values from 2e-08 to 2e-07
Outputs:
- anchor_next: float32 [4096, 512], P('fsdp', 'rep')
- momentum_next: float32 [4096, 512], P('fsdp', 'rep')
All inputs are finite; a program needn't handle non-finite values.
Results may differ from a plain program's by a relative error of at most 0.002.
Values may be sent and summed in bfloat16 or wider, within the bound.
No kernel may reach another device: no remote copies, remote signals or barrier semaphores. Data moves between devices by JAX's collectives and lax.ppermute only.
A program may use at most 64 MiB of HBM per device.

v0:
```python
import math
import jax
import jax.numpy as jnp
from jax import lax
from jax.sharding import PartitionSpec as P

beta_one = 0.9
beta_two = 0.95
adam_eps = 1e-08
inner_rate = 0.2
decay_rate = 0.1
outer_rate = 0.7
outer_mom = 0.9


def local(anchor, momentum, tokens, targets, first_moment, second_moment):
    own_columns = anchor.astype(jnp.bfloat16)
    start_rows = lax.all_gather(own_columns, "rep", axis=1, tiled=True)
    local_tokens = tokens[0]
    model_width = local_tokens.shape[1]
    groups = lax.axis_size("fsdp")
    count_tokens = local_tokens.shape[0] * groups
    columns = local_tokens
    projected = jnp.dot(
        columns,
        lax.all_gather(start_rows, "fsdp", axis=0, tiled=True),
        preferred_element_type=jnp.float32,
    )
    projected = projected * model_width ** (-0.5)
    residual = (projected - targets[0].astype(jnp.float32)).astype(jnp.bfloat16)
    columns = local_tokens
    summed = lax.psum_scatter(
        lax.dot_general(
            columns, residual, (((0,), (0,)), ((), ())), preferred_element_type=jnp.float32
        ).astype(jnp.bfloat16),
        "fsdp",
        scatter_dimension=0,
        tiled=True,
    ).astype(jnp.float32)
    gradient = summed * (1.0 / (math.sqrt(model_width) * count_tokens))
    moment_one = beta_one * first_moment[0] + (1.0 - beta_one) * gradient
    moment_two = beta_two * second_moment[0] + (1.0 - beta_two) * gradient * gradient
    direction = moment_one / (jnp.sqrt(moment_two) + adam_eps)
    update_delta = inner_rate * (direction + decay_rate * start_rows.astype(jnp.float32))
    owned_count = anchor.shape[1]
    total = lax.psum(update_delta, "rep")
    owned_sum = lax.dynamic_slice_in_dim(total, lax.axis_index("rep") * owned_count, owned_count, 1)
    mean_delta = owned_sum / lax.axis_size("rep")
    momentum_next = outer_mom * momentum + mean_delta
    anchor_next = anchor - outer_rate * (mean_delta + outer_mom * momentum_next)
    return (anchor_next, momentum_next)


def solution(mesh):
    placed = (
        P("fsdp", "rep"),
        P("fsdp", "rep"),
        P("rep", "fsdp", None),
        P("rep", "fsdp", None),
        P("rep", "fsdp", None),
        P("rep", "fsdp", None),
    )
    return jax.shard_map(
        local,
        mesh=mesh,
        in_specs=placed,
        out_specs=(P("fsdp", "rep"), P("fsdp", "rep")),
        check_vma=False,
    )
```

profile of v0, /device:TPU:1, one launch (start us, length us, event | category | flops | bytes accessed | tf_op | source)
XLA Modules:
  0.0 863.5 jit_solution(5334465605169246126)
XLA Ops:
  7.2 0.0 copy-start
  7.2 0.0 all-gather.2.cloned.1.call-start
  7.2 0.9 convert_element_type.24
  8.1 96.5 %all_gather.6 = bf16[512,512]{0,1:T(8,128)(2,1)} all-gather(bf16[512,8]{0,1:T(8,128)(2,1)S(1)} %convert_element_type.24), channel_id=1, replica_groups=mesh['rep'=64,'fsdp'=8] {'rep'}, dimensions={1}, use_global_device_ids=true | all-gather | bytes 532480 | tf_op jit(solution)/shard_map/all_gather | solution.py:18
  104.6 0.0 all-gather.2.cloned.1.call-update
  104.6 0.0 reduce-scatter.2.cloned.1.call-start
  104.6 87.4 %all-gather.2.cloned.1.call-done = bf16[4096,512]{0,1:T(8,128)(2,1)} async-done(((bf16[512,512]{0,1:T(8,128)(2,1)}), bf16[4096,512]{0,1:T(8,128)(2,1)}) %all-gather.2.cloned.1.call-update) | async-done | bytes 4194320 | tf_op jit(solution)/shard_map/all_gather | solution.py:26
  192.1 0.0 copy-done
  192.1 6.7 fusion
  198.8 0.0 copy-start.1
  198.8 0.0 reduce-scatter.2.cloned.1.call-update
  198.8 0.0 all-reduce.2.cloned.1.call-start
  198.9 2.6 copy.9
  201.5 0.0 copy-start.2
  201.5 0.0 copy-start.3
  201.5 2.5 copy.8
  204.0 91.6 %reduce-scatter.2.cloned.1.call-done = bf16[512,512]{0,1:T(8,128)(2,1)} async-done(((bf16[4096,512]{0,1:T(8,128)(2,1)}), bf16[512,512]{0,1:T(8,128)(2,1)}) %reduce-scatter.2.cloned.1.call-update) | async-done | bytes 524304 | tf_op jit(solution)/shard_map/reduce_scatter | solution.py:32
  295.6 0.0 copy-done.1
  295.6 3.5 fusion.18
  299.1 0.0 all-reduce.2.cloned.1.call-update
  299.1 556.5 %all-reduce.2.cloned.1.call-done = f32[512,512]{0,1:T(8,128)} async-done(((f32[512,512]{0,1:T(8,128)}), f32[512,512]{0,1:T(8,128)}) %all-reduce.2.cloned.1.call-update) | async-done | bytes 1048592 | tf_op jit(solution)/shard_map/psum | solution.py:46
  855.6 0.0 copy-done.2
  855.7 0.0 copy-done.3
  855.7 1.3 multiply_subtract_fusion
Async XLA Ops:
  7.2 184.9 %copy-start = (bf16[1,256,4096]{2,1,0:T(8,128)(2,1)S(1)}, bf16[1,256,4096]{2,1,0:T(8,128)(2,1)}, u32[]{:S(2)}) copy-start(bf16[1,256,4096]{2,1,0:T(8,128)(2,1)} %param.8) | copy-start | bytes 6291460
  7.2 184.9 %all-gather.2.cloned.1.call-start = ((), (), s32[]{:S(2)}) async-start(), calls=%async_computation.1 | async-start | bytes 4718592 | tf_op jit(solution)/shard_map/all_gather | solution.py:26
  104.6 191.0 %reduce-scatter.2.cloned.1.call-start = ((), (), s32[]{:S(2)}) async-start(), calls=%async_computation.2 | async-start | bytes 4718592 | tf_op jit(solution)/shard_map/reduce_scatter | solution.py:32
  198.8 96.8 %copy-start.1 = (bf16[512,512]{0,1:T(8,128)(2,1)S(1)}, bf16[512,512]{0,1:T(8,128)(2,1)}, u32[]{:S(2)}) copy-start(bf16[512,512]{0,1:T(8,128)(2,1)} %all_gather.6) | copy-start | bytes 1572868
  198.8 656.8 %all-reduce.2.cloned.1.call-start = ((), (), s32[]{:S(2)}) async-start(), calls=%async_computation.3 | async-start | bytes 2097152 | tf_op jit(solution)/shard_map/psum | solution.py:46
  201.5 654.2 %copy-start.2 = (f32[512,8]{0,1:T(8,128)S(1)}, f32[512,8]{0,1:T(8,128)}, u32[]{:S(2)}) copy-start(f32[512,8]{0,1:T(8,128)} %param.6) | copy-start | bytes 49156
  201.5 654.2 %copy-start.3 = (f32[512,8]{0,1:T(8,128)S(1)}, f32[512,8]{0,1:T(8,128)}, u32[]{:S(2)}) copy-start(f32[512,8]{0,1:T(8,128)} %param.7) | copy-start | bytes 49156
Sparse Core Ops, SparseCore 0:
  104.7 87.3 all-gather.1
  198.9 96.6 reduce-scatter.1
  299.3 556.3 all-reduce.1
where the time goes:
time: 864 us
  waiting for transfers between devices  736 us (85%)
  blocking collectives  96.5 us (11%)
  between operations  13.8 us (2%)
    psum x1, waiting for transfers between devices, local(): total = lax.psum(update_delta, 'rep')  557 us
    all_gather x1, blocking collectives, local(): start_rows = lax.all_gather(own_columns, 'rep', axis=1, tiled=True)  96.5 us
    reduce_scatter x1, waiting for transfers between devices, local(): lax.psum_scatter(lax.dot_general(columns, residual, (((0,), (0,)), ((), (...  91.6 us
    all_gather x1, waiting for transfers between devices, local(): lax.all_gather(start_rows, 'fsdp', axis=0, tiled=True)  87.4 us
  transfers between devices with their start and end apart: 3, of which 3 were waited for; matrix products, arithmetic and copies ran while one was open for 1% of the time, Pallas kernels for 0%

commit v1 on v0

--- a/solution.py
+++ b/solution.py
@@ -3,6 +3,7 @@
 import jax.numpy as jnp
 from jax import lax
 from jax.sharding import PartitionSpec as P
+from jax.lax import all_to_all, axis_size
 
 beta_one = 0.9
 beta_two = 0.95
@@ -13,6 +14,13 @@
 outer_mom = 0.9
 
 
+def _arrange_zone(xin, array_dim):
+    tmp = jnp.concatenate(
+        all_to_all(jnp.stack([xin] * axis_size("fsdp"), axis=0), "fsdp", 0, 0), axis=array_dim
+    )
+    return tmp
+
+
 def local(anchor, momentum, tokens, targets, first_moment, second_moment):
     own_columns = anchor.astype(jnp.bfloat16)
     start_rows = lax.all_gather(own_columns, "rep", axis=1, tiled=True)
@@ -21,11 +29,7 @@
     groups = lax.axis_size("fsdp")
     count_tokens = local_tokens.shape[0] * groups
     columns = local_tokens
-    projected = jnp.dot(
-        columns,
-        lax.all_gather(start_rows, "fsdp", axis=0, tiled=True),
-        preferred_element_type=jnp.float32,
-    )
+    projected = jnp.dot(columns, _arrange_zone(start_rows, 0), preferred_element_type=jnp.float32)
     projected = projected * model_width ** (-0.5)
     residual = (projected - targets[0].astype(jnp.float32)).astype(jnp.bfloat16)
     columns = local_tokens

time: 864 us -> 816 us (0.944)
  waiting for transfers between devices: 736 us -> 638 us
  blocking collectives: 96.5 us -> 145 us
    all_gather x1 -> x0, waiting for transfers between devices: 87.4 us -> none  [local(): lax.all_gather(start_rows, 'fsdp', axis=0, tiled=True)]
    all_to_all x0 -> x1, blocking collectives: none -> 54 us  [_arrange_zone(): all_to_all(jnp.stack([xin] * axis_size('fsdp'), axis=0), 'fsdp', 0, 0)]
    reduce_scatter x1, waiting for transfers between devices: 91.6 us -> 81.5 us  [local(): lax.psum_scatter(lax.dot_general(columns, residual, (((0,), (0,)), ((), (...]
  transfers between devices with their start and end apart: 3 -> 2, of which waited for: 3 -> 2; matrix products, arithmetic and copies ran while one was open for 1% -> 1% of each run, Pallas kernels for 0% -> 0%
where the time goes in v1:
time: 816 us
  waiting for transfers between devices  638 us (78%)
  blocking collectives  145 us (18%)
  between operations  14.1 us (2%)
    psum x1, waiting for transfers between devices, local(): total = lax.psum(update_delta, 'rep')  557 us
    all_gather x1, blocking collectives, local(): start_rows = lax.all_gather(own_columns, 'rep', axis=1, tiled=True)  91.3 us
    reduce_scatter x1, waiting for transfers between devices, local(): lax.psum_scatter(lax.dot_general(columns, residual, (((0,), (0,)), ((), (...  81.5 us
    all_to_all x1, blocking collectives, _arrange_zone(): all_to_all(jnp.stack([xin] * axis_size('fsdp'), axis=0), 'fsdp', 0, 0)  54 us
  transfers between devices with their start and end apart: 2, of which 2 were waited for; matrix products, arithmetic and copies ran while one was open for 1% of the time, Pallas kernels for 0%

profile of v1, /device:TPU:1, one launch (start us, length us, event | category | flops | bytes accessed | tf_op | source)
XLA Modules:
  0.0 815.8 jit_solution(17300351686176064336)
XLA Ops:
  7.2 0.0 copy-start
  7.2 0.0 reduce-scatter.2.cloned.1.call-start
  7.2 0.9 convert_element_type.24
  8.1 91.3 %all_gather.3 = bf16[512,512]{0,1:T(8,128)(2,1)S(1)} all-gather(bf16[512,8]{0,1:T(8,128)(2,1)S(1)} %convert_element_type.24), channel_id=1, replica_groups=mesh['rep'=64,'fsdp'=8] {'rep'}, dimensions={1}, use_global_device_ids=true | all-gather | bytes 532480 | tf_op jit(solution)/shard_map/all_gather | solution.py:26
  99.4 0.2 copy.9
  99.6 0.4 stack.2
  99.9 0.0 copy-start.1
  100.0 54.0 %all_to_all.5 = bf16[8,512,512]{2,1,0:T(8,128)(2,1)} all-to-all(bf16[8,512,512]{2,1,0:T(8,128)(2,1)S(1)} %stack.2), channel_id=1, replica_groups=mesh['rep'=64,'fsdp'=8] {'fsdp'}, dimensions={0} | all-to-all | bytes 8388608 | tf_op jit(solution)/shard_map/all_to_all | solution.py:19
  154.0 0.0 copy-done
  154.0 0.0 copy-done.1
  154.0 6.6 fusion
  160.6 0.0 reduce-scatter.2.cloned.1.call-update
  160.7 0.0 all-reduce.2.cloned.1.call-start
  160.7 2.6 copy.10
  163.3 0.0 copy-start.2
  163.3 0.0 copy-start.3
  163.3 2.6 copy.8
  165.8 81.5 %reduce-scatter.2.cloned.1.call-done = bf16[512,512]{0,1:T(8,128)(2,1)} async-done(((bf16[4096,512]{0,1:T(8,128)(2,1)}), bf16[512,512]{0,1:T(8,128)(2,1)}) %reduce-scatter.2.cloned.1.call-update) | async-done | bytes 524304 | tf_op jit(solution)/shard_map/reduce_scatter | solution.py:36
  247.3 3.5 fusion.18
  250.8 0.0 all-reduce.2.cloned.1.call-update
  250.8 556.8 %all-reduce.2.cloned.1.call-done = f32[512,512]{0,1:T(8,128)} async-done(((f32[512,512]{0,1:T(8,128)}), f32[512,512]{0,1:T(8,128)}) %all-reduce.2.cloned.1.call-update) | async-done | bytes 1048592 | tf_op jit(solution)/shard_map/psum | solution.py:50
  807.6 0.0 copy-done.2
  807.6 0.0 copy-done.3
  807.6 1.3 multiply_subtract_fusion
Async XLA Ops:
  7.2 146.8 %copy-start = (bf16[1,256,4096]{2,1,0:T(8,128)(2,1)S(1)}, bf16[1,256,4096]{2,1,0:T(8,128)(2,1)}, u32[]{:S(2)}) copy-start(bf16[1,256,4096]{2,1,0:T(8,128)(2,1)} %param.8) | copy-start | bytes 6291460
  7.2 240.1 %reduce-scatter.2.cloned.1.call-start = ((), (), s32[]{:S(2)}) async-start(), calls=%async_computation.2 | async-start | bytes 4718592 | tf_op jit(solution)/shard_map/reduce_scatter | solution.py:36
  99.9 54.0 %copy-start.1 = (bf16[1,256,512]{2,1,0:T(8,128)(2,1)S(1)}, bf16[1,256,512]{2,1,0:T(8,128)(2,1)}, u32[]{:S(2)}) copy-start(bf16[1,256,512]{2,1,0:T(8,128)(2,1)} %param.9) | copy-start | bytes 786436
  160.7 646.9 %all-reduce.2.cloned.1.call-start = ((), (), s32[]{:S(2)}) async-start(), calls=%async_computation.3 | async-start | bytes 2097152 | tf_op jit(solution)/shard_map/psum | solution.py:50
  163.3 644.3 %copy-start.2 = (f32[512,8]{0,1:T(8,128)S(1)}, f32[512,8]{0,1:T(8,128)}, u32[]{:S(2)}) copy-start(f32[512,8]{0,1:T(8,128)} %param.6) | copy-start | bytes 49156
  163.3 644.3 %copy-start.3 = (f32[512,8]{0,1:T(8,128)S(1)}, f32[512,8]{0,1:T(8,128)}, u32[]{:S(2)}) copy-start(f32[512,8]{0,1:T(8,128)} %param.7) | copy-start | bytes 49156
Sparse Core Ops, SparseCore 0:
  160.8 86.4 reduce-scatter.1
  250.9 556.5 all-reduce.1
